TPU v7x, 512 devices: a whole 4x8x8 slice. The times are simulated.
512 devices in a mesh: req: 128 (over z, x_hi, y), tensor: 4 (over x_lo, core).
Axes of the slice: x: 4 (x_hi: 2, x_lo: 2; x = x_hi * 2 + x_lo), y: 8, z: 8, core: 2. Of those that a mesh axis runs over, the one named last changes fastest.
Arguments:
- tokens: bfloat16 [32768, 2048], P('req'), may hold values from -6 to 6
- segment_ids: int32 [128, 256], P('req'), may hold values from 0 to 7, never falling along the last dimension, each value on 1 to 128 neighbouring positions
- padding: int32 [32768], P('req'), may hold values 0 or 1
- attn_experts: int32 [32768, 2], P('req'), may hold values from 0 to 3, all different within a row
- gain: float32 [2048], replicated, may hold values from 0.1 to 1.9
- w_router: float32 [2048, 4], replicated, may hold values from -0.125 to 0.125
- w_query: bfloat16 [2048, 4096], P('req', 'tensor'), may hold values from -1 to 1
- w_kv: bfloat16 [2048, 2048], P('req', 'tensor'), may hold values from -1 to 1
- w_out: bfloat16 [4096, 2048], P('tensor', 'req'), may hold values from -0.1875 to 0.1875
- page_shift: int32 [16], replicated, may hold values from 0 to 15, as said below
Outputs:
- attended: bfloat16 [32768, 2048], P('req', 'tensor')
- kv_cache: bfloat16 [2048, 16, 2048], P('req', None, 'tensor')
Inputs may be any that keep to these rules, and one draw needn't show every extreme that they name: `segment_ids`: segment ids never fall along a batch; each of the 8 prompts holds at least one token and at most 128. `attn_experts`: the two experts of a token differ. Block j of every batch goes to the owner page_shift[j] places further along req, cyclically, into that owner's block j.
All inputs are finite; a program needn't handle non-finite values. No bound on the sum of `padding` on one device may be relied on, other than what follows from the above.
Results may differ from a plain program's by a relative error of at most 0.013.
Values may be sent and summed in bfloat16 or wider, within the bound.
A program may use at most 64 MiB of HBM per device.

v0:
```python
import jax
import jax.numpy as jnp
from jax import lax
from jax.sharding import PartitionSpec as P

HD = 128
EXPERTS = 4
BITS = 4


def from_behind(value, axis, steps):
    count = lax.axis_size(axis)
    pairs = [(source, (source + steps) % count) for source in range(count)]
    return lax.ppermute(value, axis, pairs)


def rotate(values, position):
    half_size = values.shape[-1] // 2
    freqs = 10000.0 ** (-jnp.arange(half_size, dtype=jnp.float32) / half_size)
    angles = position.astype(jnp.float32)[:, None] * freqs[None, :]
    angles = angles.reshape((values.shape[0],) + (1,) * (values.ndim - 2) + (half_size,))
    cosine = jnp.cos(angles)
    sine = jnp.sin(angles)
    first = values[..., :half_size]
    second = values[..., half_size:]
    return jnp.concatenate(
        [first * cosine - second * sine, second * cosine + first * sine], axis=-1
    )


def allowed_mask(seg_row, pad_row, query_index, key_index):
    allowed = (seg_row[query_index][:, None] == seg_row[key_index][None, :]) & (
        key_index[None, :] <= query_index[:, None]
    )
    return allowed & (
        (pad_row[key_index][None, :] == 1) | (key_index[None, :] == query_index[:, None])
    )


def attend_dense(queries, keys, values, seg_row, pad_row):
    count = queries.shape[0]
    index = jnp.arange(count, dtype=jnp.int32)
    allowed = allowed_mask(seg_row, pad_row, index, index)
    scores = jnp.einsum(
        "tshd,uhd->shtu", queries, keys, preferred_element_type=jnp.float32
    ) / jnp.sqrt(jnp.float32(queries.shape[-1]))
    masked = jnp.where(allowed[None, None], scores, -1e30)
    peak = jnp.max(masked, axis=3, keepdims=True)
    weights = jnp.where(allowed[None, None], jnp.exp(masked - peak), 0.0)
    total = jnp.sum(weights, axis=3)
    summed = jnp.einsum(
        "shtu,uhd->tshd", weights.astype(jnp.bfloat16), values, preferred_element_type=jnp.float32
    )
    return summed / jnp.transpose(total, (2, 0, 1))[:, :, :, None]


def on_device(
    tokens, segment_ids, padding, attn_experts, gain, w_router, w_query, w_kv, w_out, page_shift
):
    count = tokens.shape[0]
    seg_row = segment_ids[0]
    starts = jnp.sum((seg_row[None, :] < seg_row[:, None]).astype(jnp.int32), axis=1)
    position = jnp.arange(count, dtype=jnp.int32) - starts
    x_float = tokens.astype(jnp.float32)
    normed = (
        x_float
        * lax.rsqrt(jnp.mean(x_float * x_float, axis=1, keepdims=True) + 1e-06)
        * gain[None, :]
    ).astype(jnp.bfloat16)
    pad_float = padding.astype(jnp.float32)
    local_heads = w_kv.shape[1] // (2 * HD)

    def add_rows(piece):
        return jnp.dot(normed, piece, preferred_element_type=jnp.float32)

    keyval = add_rows(lax.all_gather(w_kv, "req", axis=0, tiled=True))
    query_all = add_rows(lax.all_gather(w_query, "req", axis=0, tiled=True))
    keyval = keyval.reshape(count, local_heads, 2, HD)
    keys_rot = rotate(keyval[:, :, 0, :], position)
    keyval = (
        jnp.stack([keys_rot, keyval[:, :, 1, :]], axis=2) * pad_float[:, None, None, None]
    ).astype(jnp.bfloat16)
    logits = jnp.dot(normed.astype(jnp.float32), w_router, preferred_element_type=jnp.float32)
    selector = (
        attn_experts[:, :, None] == jnp.arange(EXPERTS, dtype=jnp.int32)[None, None, :]
    ).astype(jnp.float32)
    gates = jnp.einsum("tse,te->ts", selector, jax.nn.sigmoid(logits))
    query_all = rotate(query_all.reshape(count, local_heads, EXPERTS, HD), position)
    queries = jnp.einsum("thed,tse->tshd", query_all, selector).astype(jnp.bfloat16)
    keys_b = keyval[:, :, 0, :]
    values_b = keyval[:, :, 1, :]
    heads_out = attend_dense(queries, keys_b, values_b, seg_row, padding)
    mixed = (
        jnp.einsum("tshd,tse->thed", heads_out * gates[:, :, None, None], selector)
        * pad_float[:, None, None, None]
    )
    mixed = mixed.reshape(count, local_heads * EXPERTS * HD).astype(jnp.bfloat16)
    partial_out = jnp.dot(
        mixed, lax.all_gather(w_out, "req", axis=1, tiled=True), preferred_element_type=jnp.float32
    )
    attended = lax.psum_scatter(
        partial_out.astype(jnp.bfloat16), "tensor", scatter_dimension=1, tiled=True
    )
    page_count = page_shift.shape[0]
    page_size = count // page_count
    pages = keyval.reshape(page_count, page_size, local_heads * 2 * HD)
    for level in range(BITS):
        moved = from_behind(pages, "req", 2**level)
        taken = page_shift // 2**level % 2 == 1
        pages = jnp.where(taken[:, None, None], moved, pages)
    return (attended, pages)


def solution(mesh):
    placed = (
        P("req", None),
        P("req", None),
        P("req"),
        P("req", None),
        P(),
        P(),
        P("req", "tensor"),
        P("req", "tensor"),
        P("tensor", "req"),
        P(),
    )
    return jax.shard_map(
        on_device,
        mesh=mesh,
        in_specs=placed,
        out_specs=(P("req", "tensor"), P("req", None, "tensor")),
        check_vma=False,
    )
```

profile of v0, /device:TPU:2, one launch (start us, length us, event | category | flops | bytes accessed | tf_op | source)
XLA Modules:
  0.0 492.8 jit_solution(6888651575733452197)
XLA Ops:
  7.2 0.7 all-gather.4.cloned.1.call-update
  8.0 0.7 all-gather.6.cloned.1.call-update
  8.7 0.7 all-gather.8.cloned.1.call-update
  9.5 0.7 convert_element_type.50
  10.2 0.8 copy.27
  11.1 2.0 gather_fusion.1
  13.1 2.0 gather_fusion
  15.1 0.3 fusion.1
  15.4 0.5 fusion.15
  15.8 0.2 copy.48
  16.0 0.9 fusion.22
  17.0 0.2 convert_reduce_fusion
  17.2 0.1 fusion.25
  17.3 0.5 multiply_cosine_fusion
  17.9 127.1 %all-gather.4.cloned.1.call-done = bf16[2048,512]{1,0:T(8,128)(2,1)} async-done(((bf16[16,512]{1,0:T(8,128)(2,1)}), bf16[2048,512]{1,0:T(8,128)(2,1)}) %all-gather.4.cloned.1.call-update) | async-done | bytes 2097168 | tf_op jit(solution)/shard_map/all_gather | solution.py:76
  145.0 2.3 fusion.46
  147.3 0.3 reshape.219
  147.6 0.4 fusion.48
  148.1 0.2 multiply_subtract_fusion.1
  148.3 0.1 maximum_bitcast_fusion
  148.4 0.1 pad_maximum_fusion
  148.5 0.4 copy.34
  149.0 0.4 stack.10
  149.4 133.6 %all-gather.6.cloned.1.call-done = bf16[2048,1024]{1,0:T(8,128)(2,1)} async-done(((bf16[16,1024]{1,0:T(8,128)(2,1)}), bf16[2048,1024]{1,0:T(8,128)(2,1)}) %all-gather.6.cloned.1.call-update) | async-done | bytes 4194320 | tf_op jit(solution)/shard_map/all_gather | solution.py:77
  283.0 3.5 fusion.44
  286.5 0.5 reshape.220
  287.0 0.8 multiply_subtract_fusion
  287.8 1.2 convolution_convert_fusion.1
  289.0 0.6 fusion.49
  289.6 0.3 fusion.8
  289.9 0.4 fusion.12
  290.4 0.2 copy.33
  290.5 1.4 fusion.10
  292.0 0.4 convert_element_type.56
  292.3 128.7 %all-gather.8.cloned.1.call-done = bf16[1024,2048]{0,1:T(8,128)(2,1)} async-done(((bf16[1024,16]{0,1:T(8,128)(2,1)}), bf16[1024,2048]{0,1:T(8,128)(2,1)}) %all-gather.8.cloned.1.call-update) | async-done | bytes 4194320 | tf_op jit(solution)/shard_map/all_gather | solution.py:99
  421.0 4.4 convolution_convert_fusion
  425.5 0.1 multiply_convert_fusion
  425.6 2.9 collective-permute-start
  428.6 11.1 %collective-permute-done = bf16[16,16,512]{2,1,0:T(8,128)(2,1)S(1)} collective-permute-done((bf16[16,16,512]{2,1,0:T(8,128)(2,1)S(1)}, bf16[16,16,512]{2,1,0:T(8,128)(2,1)S(1)}, u32[]{:S(2)}, u32[]{:S(2)}) %collective-permute-start) | collective-permute-done | bytes 262176 | tf_op jit(solution)/shard_map/ppermute | solution.py:14
  439.7 0.1 broadcast_select_fusion
  439.9 1.9 collective-permute-start.1
  441.8 13.0 %collective-permute-done.1 = bf16[16,16,512]{2,1,0:T(8,128)(2,1)S(1)} collective-permute-done((bf16[16,16,512]{2,1,0:T(8,128)(2,1)S(1)}, bf16[16,16,512]{2,1,0:T(8,128)(2,1)S(1)}, u32[]{:S(2)}, u32[]{:S(2)}) %collective-permute-start.1) | collective-permute-done | bytes 262176 | tf_op jit(solution)/shard_map/ppermute | solution.py:14
  454.7 0.1 broadcast_select_fusion.1
  454.8 1.9 collective-permute-start.2
  456.8 16.3 %collective-permute-done.2 = bf16[16,16,512]{2,1,0:T(8,128)(2,1)S(1)} collective-permute-done((bf16[16,16,512]{2,1,0:T(8,128)(2,1)S(1)}, bf16[16,16,512]{2,1,0:T(8,128)(2,1)S(1)}, u32[]{:S(2)}, u32[]{:S(2)}) %collective-permute-start.2) | collective-permute-done | bytes 262176 | tf_op jit(solution)/shard_map/ppermute | solution.py:14
  473.2 1.9 collective-permute-start.3
  475.1 10.4 %collective-permute-done.3 = bf16[16,16,512]{2,1,0:T(8,128)(2,1)S(1)} collective-permute-done((bf16[16,16,512]{2,1,0:T(8,128)(2,1)S(1)}, bf16[16,16,512]{2,1,0:T(8,128)(2,1)S(1)}, u32[]{:S(2)}, u32[]{:S(2)}) %collective-permute-start.3) | collective-permute-done | bytes 262176 | tf_op jit(solution)/shard_map/ppermute | solution.py:14
  485.5 0.8 broadcast_select_fusion.3
  (28 shorter events, 0.5 us)
Async XLA Ops:
  7.2 8.2 %copy-start = (f32[2048,4]{0,1:T(4,128)S(1)}, f32[2048,4]{0,1:T(4,128)}, u32[]{:S(2)}) copy-start(f32[2048,4]{0,1:T(4,128)} %param.15) | copy-start | bytes 98308
  7.2 7.9 %copy-start.2 = (bf16[256,2048]{1,0:T(8,128)(2,1)S(1)}, bf16[256,2048]{1,0:T(8,128)(2,1)}, u32[]{:S(2)}) copy-start(bf16[256,2048]{1,0:T(8,128)(2,1)} %param.10) | copy-start | bytes 3145732
  7.2 8.2 %copy-start.4 = (f32[2048]{0:T(1024)S(1)}, f32[2048]{0:T(1024)}, u32[]{:S(2)}) copy-start(f32[2048]{0:T(1024)} %param.14) | copy-start | bytes 24580
  7.2 137.8 %all-gather.4.cloned.1.call-start = ((), (), s32[]{:S(2)}) async-start(), calls=%async_computation.1 | async-start | bytes 2113536 | tf_op jit(solution)/shard_map/all_gather | solution.py:76
  7.9 275.1 %all-gather.6.cloned.1.call-start = ((), (), s32[]{:S(2)}) async-start(), calls=%async_computation.2 | async-start | bytes 4227072 | tf_op jit(solution)/shard_map/all_gather | solution.py:77
  8.7 412.3 %all-gather.8.cloned.1.call-start = ((), (), s32[]{:S(2)}) async-start(), calls=%async_computation.3 | async-start | bytes 4227072 | tf_op jit(solution)/shard_map/all_gather | solution.py:99
  9.4 476.9 %reduce-scatter.2.cloned.1.call-start = ((), (), s32[]{:S(2)}) async-start(), calls=%async_computation.4 | async-start | bytes 1310720 | tf_op jit(solution)/shard_map/reduce_scatter | solution.py:101
  15.0 1.9 copy-start.1
  292.3 136.2 %copy-start.3 = (s32[16]{0:T(128)S(1)}, s32[16]{0:T(128)}, u32[]{:S(2)}) copy-start(s32[16]{0:T(128)} %param.19) | copy-start | bytes 196
  425.6 14.1 %collective-permute-start = (bf16[16,16,512]{2,1,0:T(8,128)(2,1)S(1)}, bf16[16,16,512]{2,1,0:T(8,128)(2,1)S(1)}, u32[]{:S(2)}, u32[]{:S(2)}) collective-permute-start(bf16[16,16,512]{2,1,0:T(8,128)(2,1)S(1)} %multiply_convert_fusion), channel_id=1, source_target_pairs={{0,4},{4,8},{8,12},{12,16},{16,20},{20,24},{24,28},{28,32},{32,36}... | collective-permute-start | bytes 786440 | tf_op jit(solution)/shard_map/ppermute | solution.py:14
  439.9 14.9 %collective-permute-start.1 = (bf16[16,16,512]{2,1,0:T(8,128)(2,1)S(1)}, bf16[16,16,512]{2,1,0:T(8,128)(2,1)S(1)}, u32[]{:S(2)}, u32[]{:S(2)}) collective-permute-start(bf16[16,16,512]{2,1,0:T(8,128)(2,1)S(1)} %broadcast_select_fusion), channel_id=1, source_target_pairs={{0,8},{4,12},{8,16},{12,20},{16,24},{20,28},{24,32},{28,36},{32,40... | collective-permute-start | bytes 786440 | tf_op jit(solution)/shard_map/ppermute | solution.py:14
  454.8 18.2 %collective-permute-start.2 = (bf16[16,16,512]{2,1,0:T(8,128)(2,1)S(1)}, bf16[16,16,512]{2,1,0:T(8,128)(2,1)S(1)}, u32[]{:S(2)}, u32[]{:S(2)}) collective-permute-start(bf16[16,16,512]{2,1,0:T(8,128)(2,1)S(1)} %broadcast_select_fusion.1), channel_id=1, source_target_pairs={{0,16},{4,20},{8,24},{12,28},{16,32},{20,36},{24,40},{28,44},{32,4... | collective-permute-start | bytes 786440 | tf_op jit(solution)/shard_map/ppermute | solution.py:14
  473.2 12.3 %collective-permute-start.3 = (bf16[16,16,512]{2,1,0:T(8,128)(2,1)S(1)}, bf16[16,16,512]{2,1,0:T(8,128)(2,1)S(1)}, u32[]{:S(2)}, u32[]{:S(2)}) collective-permute-start(bf16[16,16,512]{2,1,0:T(8,128)(2,1)S(1)} %broadcast_select_fusion.2), channel_id=1, source_target_pairs={{0,32},{4,36},{8,40},{12,44},{16,48},{20,52},{24,56},{28,60},{32,6... | collective-permute-start | bytes 786440 | tf_op jit(solution)/shard_map/ppermute | solution.py:14
Sparse Core Ops, SparseCore 0:
  12.5 132.3 all-gather.3
  149.3 133.6 all-gather.5
  287.4 133.5 all-gather.7
  425.6 23.1 reduce-scatter.1
where the time goes:
time: 493 us
  waiting for transfers between devices  442 us (90%)
  matrix products  14.7 us (3%)
  between operations  14.1 us (3%)
  starting transfers between devices  8.84 us (2%)
  local copies, waits for them, and re-layouts  7.76 us (2%)
  other arithmetic  5.18 us (1%)
    all_gather x1, waiting for transfers between devices, on_device(): query_all = add_rows(lax.all_gather(w_query, 'req', axis=0, tiled=True))  134 us
    all_gather x1, waiting for transfers between devices, on_device(): lax.all_gather(w_out, 'req', axis=1, tiled=True)  129 us
    all_gather x1, waiting for transfers between devices, on_device(): keyval = add_rows(lax.all_gather(w_kv, 'req', axis=0, tiled=True))  127 us
    ppermute x4, waiting for transfers between devices, from_behind(): return lax.ppermute(value, axis, pairs)  50.8 us
  transfers between devices with their start and end apart: 8, of which 7 were waited for; matrix products, arithmetic and copies ran while one was open for 5% of the time, Pallas kernels for 0%

commit v1 on v0

--- a/solution.py
+++ b/solution.py
@@ -73,7 +73,14 @@
     def add_rows(piece):
         return jnp.dot(normed, piece, preferred_element_type=jnp.float32)
 
-    keyval = add_rows(lax.all_gather(w_kv, "req", axis=0, tiled=True))
+    keyval = add_rows(
+        jnp.concatenate(
+            lax.all_to_all(
+                jnp.stack(lax.axis_size("req") * [w_kv]), "req", split_axis=0, concat_axis=0
+            ),
+            0,
+        )
+    )
     query_all = add_rows(lax.all_gather(w_query, "req", axis=0, tiled=True))
     keyval = keyval.reshape(count, local_heads, 2, HD)
     keys_rot = rotate(keyval[:, :, 0, :], position)

time: 493 us -> 395 us (0.80)
  waiting for transfers between devices: 442 us -> 317 us
  starting transfers between devices: 8.84 us -> 28.5 us
  local copies, waits for them, and re-layouts: 7.76 us -> 14.5 us
    all_gather x1 -> x0, waiting for transfers between devices: 127 us -> none  [on_device(): keyval = add_rows(lax.all_gather(w_kv, 'req', axis=0, tiled=True))]
    all_to_all x0 -> x1, waiting for transfers between devices: none -> 43.5 us  [on_device(): lax.all_to_all(jnp.stack(lax.axis_size('req') * [w_kv]), 'req', split_axi...]
    all_gather x1, waiting for transfers between devices: 134 us -> 93.2 us  [on_device(): query_all = add_rows(lax.all_gather(w_query, 'req', axis=0, tiled=True))]
    all_to_all x0 -> x1, starting transfers between devices: none -> 19.5 us  [on_device(): lax.all_to_all(jnp.stack(lax.axis_size('req') * [w_kv]), 'req', split_axi...]
  transfers between devices with their start and end apart: 8 -> 8, of which waited for: 7 -> 7; matrix products, arithmetic and copies ran while one was open for 5% -> 8% of each run, Pallas kernels for 0% -> 0%
where the time goes in v1:
time: 395 us; the launch traced here: 394 us
  waiting for transfers between devices  317 us (80%)
  starting transfers between devices  28.5 us (7%)
  matrix products  14.9 us (4%)
  local copies, waits for them, and re-layouts  14.5 us (4%)
  between operations  14.1 us (4%)
  other arithmetic  5.48 us (1%)
    all_gather x1, waiting for transfers between devices, on_device(): lax.all_gather(w_out, 'req', axis=1, tiled=True)  128 us
    all_gather x1, waiting for transfers between devices, on_device(): query_all = add_rows(lax.all_gather(w_query, 'req', axis=0, tiled=True))  93.2 us
    ppermute x4, waiting for transfers between devices, from_behind(): return lax.ppermute(value, axis, pairs)  50.8 us
    all_to_all x1, waiting for transfers between devices, on_device(): lax.all_to_all(jnp.stack(lax.axis_size('req') * [w_kv]), 'req', split_axi...  43.5 us
    all_to_all x1, starting transfers between devices, on_device(): lax.all_to_all(jnp.stack(lax.axis_size('req') * [w_kv]), 'req', split_axi...  19.5 us
    ppermute x4, starting transfers between devices, from_behind(): return lax.ppermute(value, axis, pairs)  8.69 us
  transfers between devices with their start and end apart: 8, of which 7 were waited for; matrix products, arithmetic and copies ran while one was open for 8% of the time, Pallas kernels for 0%

profile of v1, /device:TPU:2, one launch (start us, length us, event | category | flops | bytes accessed | tf_op | source)
XLA Modules:
  0.0 394.4 jit_solution(324088097482953899)
XLA Ops:
  7.2 0.7 all-gather.3.cloned.1.call-update
  8.0 0.7 all-gather.5.cloned.1.call-update
  8.7 2.3 stack.8
  11.0 19.5 %all-to-all-start = ((bf16[128,16,512]{2,1,0:T(8,128)(2,1)}), bf16[128,16,512]{2,1,0:T(8,128)(2,1)S(1)}, u32[]{:S(2)}, u32[]{:S(2)}) async-start(bf16[128,16,512]{2,1,0:T(8,128)(2,1)} %stack.8), calls=%async_computation | async-start | bytes 4194304 | tf_op jit(solution)/shard_map/all_to_all | solution.py:78
  30.6 0.2 reduce-scatter.2.cloned.1.call-start
  30.9 1.9 gather_fusion.1
  32.9 1.9 gather_fusion
  34.8 0.2 convert_reduce_fusion
  35.0 0.3 multiply_cosine_fusion
  35.3 0.8 copy.39
  36.1 0.8 copy.40
  36.8 0.1 copy.36
  37.0 0.3 fusion.1
  37.3 0.5 fusion.15
  37.8 0.8 copy.59
  38.6 2.4 fusion.24
  41.0 1.0 copy.55
  41.9 0.1 fusion.27
  42.1 43.5 %all-to-all-done = bf16[128,16,512]{2,1,0:T(8,128)(2,1)S(1)} async-done(((bf16[128,16,512]{2,1,0:T(8,128)(2,1)}), bf16[128,16,512]{2,1,0:T(8,128)(2,1)S(1)}, u32[]{:S(2)}, u32[]{:S(2)}) %all-to-all-start) | async-done | bytes 2097184 | tf_op jit(solution)/shard_map/all_to_all | solution.py:78
  85.6 2.5 copy.37
  88.1 2.4 fusion.19
  90.7 0.3 copy.45
  91.0 0.4 stack.11
  91.4 93.2 %all-gather.3.cloned.1.call-done = bf16[2048,1024]{1,0:T(8,128)(2,1)} async-done(((bf16[16,1024]{1,0:T(8,128)(2,1)}), bf16[2048,1024]{1,0:T(8,128)(2,1)}) %all-gather.3.cloned.1.call-update) | async-done | bytes 4194320 | tf_op jit(solution)/shard_map/all_gather | solution.py:84
  184.7 3.5 fusion.46
  188.2 0.5 reshape.224
  188.7 0.4 copy-done.4
  189.1 0.8 multiply_subtract_fusion
  189.9 1.2 convolution_convert_fusion.1
  191.1 0.6 fusion.49
  191.8 0.4 fusion.8
  192.2 0.4 fusion.12
  192.6 0.2 copy.44
  192.8 1.4 fusion.10
  194.2 0.4 convert_element_type.56
  194.6 128.1 %all-gather.5.cloned.1.call-done = bf16[1024,2048]{0,1:T(8,128)(2,1)} async-done(((bf16[1024,16]{0,1:T(8,128)(2,1)}), bf16[1024,2048]{0,1:T(8,128)(2,1)}) %all-gather.5.cloned.1.call-update) | async-done | bytes 4194320 | tf_op jit(solution)/shard_map/all_gather | solution.py:106
  322.7 4.4 %convolution_convert_fusion = bf16[256,2048]{1,0:T(8,128)(2,1)} fusion(bf16[256,1024]{1,0:T(8,128)(2,1)S(1)} %convert_element_type.56, bf16[1024,2048]{0,1:T(8,128)(2,1)} %all-gather.5.cloned.1.call-done), kind=kOutput, calls=%fused_computation.5 | convolution fusion | flops 1074266112 | bytes 5767168 | tf_op jit(solution)/shard_map/dot_general | solution.py:105
  327.1 0.1 multiply_convert_fusion
  327.2 2.9 collective-permute-start
  330.2 11.1 %collective-permute-done = bf16[16,16,512]{2,1,0:T(8,128)(2,1)S(1)} collective-permute-done((bf16[16,16,512]{2,1,0:T(8,128)(2,1)S(1)}, bf16[16,16,512]{2,1,0:T(8,128)(2,1)S(1)}, u32[]{:S(2)}, u32[]{:S(2)}) %collective-permute-start) | collective-permute-done | bytes 262176 | tf_op jit(solution)/shard_map/ppermute | solution.py:14
  341.3 0.1 broadcast_select_fusion
  341.5 1.9 collective-permute-start.1
  343.4 13.0 %collective-permute-done.1 = bf16[16,16,512]{2,1,0:T(8,128)(2,1)S(1)} collective-permute-done((bf16[16,16,512]{2,1,0:T(8,128)(2,1)S(1)}, bf16[16,16,512]{2,1,0:T(8,128)(2,1)S(1)}, u32[]{:S(2)}, u32[]{:S(2)}) %collective-permute-start.1) | collective-permute-done | bytes 262176 | tf_op jit(solution)/shard_map/ppermute | solution.py:14
  356.5 1.9 collective-permute-start.2
  358.4 16.3 %collective-permute-done.2 = bf16[16,16,512]{2,1,0:T(8,128)(2,1)S(1)} collective-permute-done((bf16[16,16,512]{2,1,0:T(8,128)(2,1)S(1)}, bf16[16,16,512]{2,1,0:T(8,128)(2,1)S(1)}, u32[]{:S(2)}, u32[]{:S(2)}) %collective-permute-start.2) | collective-permute-done | bytes 262176 | tf_op jit(solution)/shard_map/ppermute | solution.py:14
  374.8 1.9 collective-permute-start.3
  376.7 10.4 %collective-permute-done.3 = bf16[16,16,512]{2,1,0:T(8,128)(2,1)S(1)} collective-permute-done((bf16[16,16,512]{2,1,0:T(8,128)(2,1)S(1)}, bf16[16,16,512]{2,1,0:T(8,128)(2,1)S(1)}, u32[]{:S(2)}, u32[]{:S(2)}) %collective-permute-start.3) | collective-permute-done | bytes 262176 | tf_op jit(solution)/shard_map/ppermute | solution.py:14
  387.1 0.8 broadcast_select_fusion.3
  (36 shorter events, 0.7 us)
Async XLA Ops:
  7.2 30.1 %copy-start = (f32[2048,4]{0,1:T(4,128)S(1)}, f32[2048,4]{0,1:T(4,128)}, u32[]{:S(2)}) copy-start(f32[2048,4]{0,1:T(4,128)} %param.15) | copy-start | bytes 98308
  7.2 177.5 %all-gather.3.cloned.1.call-start = ((), (), s32[]{:S(2)}) async-start(), calls=%async_computation.2 | async-start | bytes 4227072 | tf_op jit(solution)/shard_map/all_gather | solution.py:84
  7.9 314.7 %all-gather.5.cloned.1.call-start = ((), (), s32[]{:S(2)}) async-start(), calls=%async_computation.3 | async-start | bytes 4227072 | tf_op jit(solution)/shard_map/all_gather | solution.py:106
  11.0 19.8 %copy-start.2 = (s32[256]{0:T(256)S(1)}, s32[256]{0:T(256)}, u32[]{:S(2)}) copy-start(s32[256]{0:T(256)} %param.12) | copy-start | bytes 3076
  11.0 21.8 %copy-start.1 = (s32[1,256]{1,0:T(1,128)S(1)}, s32[1,256]{1,0:T(1,128)}, u32[]{:S(2)}) copy-start(s32[1,256]{1,0:T(1,128)} %param.11) | copy-start | bytes 3076
  11.0 74.6 %all-to-all-start = ((bf16[128,16,512]{2,1,0:T(8,128)(2,1)}), bf16[128,16,512]{2,1,0:T(8,128)(2,1)S(1)}, u32[]{:S(2)}, u32[]{:S(2)}) async-start(bf16[128,16,512]{2,1,0:T(8,128)(2,1)} %stack.8), calls=%async_computation | async-start | bytes 4194304 | tf_op jit(solution)/shard_map/all_to_all | solution.py:78
  30.5 6.3 %copy-start.6 = (s32[256,2]{0,1:T(2,128)S(1)}, s32[256,2]{0,1:T(2,128)}, u32[]{:S(2)}) copy-start(s32[256,2]{0,1:T(2,128)} %param.13) | copy-start | bytes 6148
  30.5 6.5 %copy-start.3 = (bf16[256,2048]{1,0:T(8,128)(2,1)S(1)}, bf16[256,2048]{1,0:T(8,128)(2,1)}, u32[]{:S(2)}) copy-start(bf16[256,2048]{1,0:T(8,128)(2,1)} %param.10) | copy-start | bytes 3145732
  30.5 6.8 %copy-start.8 = (f32[2048]{0:T(1024)S(1)}, f32[2048]{0:T(1024)}, u32[]{:S(2)}) copy-start(f32[2048]{0:T(1024)} %param.14) | copy-start | bytes 24580
  30.6 357.4 %reduce-scatter.2.cloned.1.call-start = ((), (), s32[]{:S(2)}) async-start(), calls=%async_computation.4 | async-start | bytes 1310720 | tf_op jit(solution)/shard_map/reduce_scatter | solution.py:108
  188.1 0.9 copy-start.4
  188.1 1.0 copy-start.5
  194.5 135.6 %copy-start.7 = (s32[16]{0:T(128)S(1)}, s32[16]{0:T(128)}, u32[]{:S(2)}) copy-start(s32[16]{0:T(128)} %param.19) | copy-start | bytes 196
  327.2 14.1 %collective-permute-start = (bf16[16,16,512]{2,1,0:T(8,128)(2,1)S(1)}, bf16[16,16,512]{2,1,0:T(8,128)(2,1)S(1)}, u32[]{:S(2)}, u32[]{:S(2)}) collective-permute-start(bf16[16,16,512]{2,1,0:T(8,128)(2,1)S(1)} %multiply_convert_fusion), channel_id=1, source_target_pairs={{0,4},{4,8},{8,12},{12,16},{16,20},{20,24},{24,28},{28,32},{32,36}... | collective-permute-start | bytes 786440 | tf_op jit(solution)/shard_map/ppermute | solution.py:14
  341.5 14.9 %collective-permute-start.1 = (bf16[16,16,512]{2,1,0:T(8,128)(2,1)S(1)}, bf16[16,16,512]{2,1,0:T(8,128)(2,1)S(1)}, u32[]{:S(2)}, u32[]{:S(2)}) collective-permute-start(bf16[16,16,512]{2,1,0:T(8,128)(2,1)S(1)} %broadcast_select_fusion), channel_id=1, source_target_pairs={{0,8},{4,12},{8,16},{12,20},{16,24},{20,28},{24,32},{28,36},{32,40... | collective-permute-start | bytes 786440 | tf_op jit(solution)/shard_map/ppermute | solution.py:14
  356.5 18.2 %collective-permute-start.2 = (bf16[16,16,512]{2,1,0:T(8,128)(2,1)S(1)}, bf16[16,16,512]{2,1,0:T(8,128)(2,1)S(1)}, u32[]{:S(2)}, u32[]{:S(2)}) collective-permute-start(bf16[16,16,512]{2,1,0:T(8,128)(2,1)S(1)} %broadcast_select_fusion.1), channel_id=1, source_target_pairs={{0,16},{4,20},{8,24},{12,28},{16,32},{20,36},{24,40},{28,44},{32,4... | collective-permute-start | bytes 786440 | tf_op jit(solution)/shard_map/ppermute | solution.py:14
  374.8 12.3 %collective-permute-start.3 = (bf16[16,16,512]{2,1,0:T(8,128)(2,1)S(1)}, bf16[16,16,512]{2,1,0:T(8,128)(2,1)S(1)}, u32[]{:S(2)}, u32[]{:S(2)}) collective-permute-start(bf16[16,16,512]{2,1,0:T(8,128)(2,1)S(1)} %broadcast_select_fusion.2), channel_id=1, source_target_pairs={{0,32},{4,36},{8,40},{12,44},{16,48},{20,52},{24,56},{28,60},{32,6... | collective-permute-start | bytes 786440 | tf_op jit(solution)/shard_map/ppermute | solution.py:14
Sparse Core Ops, SparseCore 0:
  12.4 172.2 all-gather.2
  189.0 133.5 all-gather.4
  327.2 23.1 reduce-scatter.1
